TPU v7x, 512 devices: a whole 4x8x8 slice. The times are simulated.
512 devices in a mesh: dp: 16 (over z, core), tp: 4 (over y_lo), cp: 8 (over y_hi, x).
Axes of the slice: x: 4, y: 8 (y_hi: 2, y_lo: 4; y = y_hi * 4 + y_lo), z: 8, core: 2. Of those that a mesh axis runs over, the one named last changes fastest.
Arguments:
- tokens: bfloat16 [65536, 1024], P(('dp', 'tp', 'cp')), may hold values from -6 to 6
- expert_ids: int32 [65536, 2], P(('dp', 'tp', 'cp')), may hold values from 0 to 31, all different within a row; in each aligned block of 128 rows (0 to 127, 128 to 255, ...) at most 12 rows name the same one
- router_weight: bfloat16 [1024, 32], replicated, may hold values from -0.1875 to 0.1875
- gate_weight: bfloat16 [32, 1024, 384], P(('tp', 'cp'), 'dp'), may hold values from -0.1875 to 0.1875
- up_weight: bfloat16 [32, 1024, 384], P(('tp', 'cp'), 'dp'), may hold values from -0.1875 to 0.1875
- down_weight: bfloat16 [32, 384, 1024], P(('tp', 'cp'), None, 'dp'), may hold values from -0.3125 to 0.3125
- grad_out: bfloat16 [65536, 1024], P(('dp', 'tp', 'cp')), may hold values from -6 to 6
Outputs:
- moe_out: bfloat16 [65536, 1024], P(('dp', 'tp', 'cp'))
- grad_tokens: bfloat16 [65536, 1024], P(('dp', 'tp', 'cp'))
- router_grad: float32 [1024, 32], replicated
Inputs may be any that keep to these rules, and one draw needn't show every extreme that they name: `expert_ids`: each row names 2 different experts. Among the 128 rows of one device no expert is named by more than 12 rows, a bound that some block reaches.
All inputs are finite; a program needn't handle non-finite values.
Results may differ from a plain program's by a relative error of at most 0.0064.
Values may be sent and summed in bfloat16 or wider, within the bound.
A program may use at most 64 MiB of HBM per device.

v0:
```python
import jax
import jax.numpy as jnp
from jax import lax
from jax.sharding import PartitionSpec as P


def route_slots(flat_ids, expert_count):
    hits = (flat_ids[:, None] == jnp.arange(expert_count, dtype=jnp.int32)[None, :]).astype(
        jnp.int32
    )
    before = jnp.cumsum(hits, axis=0) - hits
    return jnp.sum(before * hits, axis=1)


def trade(stacked, capacity):
    item_count = stacked.shape[0]
    feature_dim = stacked.shape[2]
    tp_count = lax.axis_size("tp")
    cp_count = lax.axis_size("cp")
    shaped = stacked.reshape(item_count, tp_count * cp_count, capacity, feature_dim)
    moved = lax.all_to_all(shaped, ("tp", "cp"), split_axis=1, concat_axis=1, tiled=True)
    return moved.reshape(item_count, -1, feature_dim)


def expert_forward(received, w_gate, w_up, w_down):
    gate_act = jnp.dot(received, w_gate, preferred_element_type=jnp.float32)
    up_act = jnp.dot(received, w_up, preferred_element_type=jnp.float32)
    hidden = (jax.nn.silu(gate_act) * up_act).astype(jnp.bfloat16)
    produced = jnp.dot(hidden, w_down, preferred_element_type=jnp.float32).astype(jnp.bfloat16)
    return (gate_act, up_act, produced)


def expert_backward(received_grad, gate_act, up_act, w_gate, w_up, w_down):
    contract = (((1,), (1,)), ((), ()))
    grad_hidden = lax.dot_general(
        received_grad, w_down, contract, preferred_element_type=jnp.float32
    )
    sigma = jax.nn.sigmoid(gate_act)
    grad_gate = (grad_hidden * up_act * sigma * (1.0 + gate_act * (1.0 - sigma))).astype(
        jnp.bfloat16
    )
    grad_up = (grad_hidden * gate_act * sigma).astype(jnp.bfloat16)
    returned = lax.dot_general(grad_gate, w_gate, contract, preferred_element_type=jnp.float32)
    returned = returned + lax.dot_general(
        grad_up, w_up, contract, preferred_element_type=jnp.float32
    )
    return returned.astype(jnp.bfloat16)


def on_device(tokens, expert_ids, router_weight, gate_weight, up_weight, down_weight, grad_out):
    row_count, feature_dim = tokens.shape
    topk = expert_ids.shape[1]
    groups = lax.axis_size(("tp", "cp"))
    capacity = 3 * row_count * topk // (2 * groups)
    expert_count = router_weight.shape[1]
    contract = (((1,), (1,)), ((), ()))
    w_gate, w_up, w_down = (
        lax.all_gather(gate_weight[0], "dp", axis=0, tiled=True),
        lax.all_gather(up_weight[0], "dp", axis=0, tiled=True),
        lax.all_gather(down_weight[0], "dp", axis=1, tiled=True),
    )
    logits = jnp.dot(tokens, router_weight, preferred_element_type=jnp.float32)
    chosen = jnp.take_along_axis(logits, expert_ids, axis=1)
    mixing = 1.0 / jnp.sum(jnp.exp(chosen[:, None, :] - chosen[:, :, None]), axis=2)
    flat_ids = expert_ids.reshape(-1)
    slots = route_slots(flat_ids, expert_count)
    position = flat_ids * capacity + slots
    slot_total = groups * capacity
    repeated = jnp.repeat(tokens, topk, axis=0)
    scaled_grad = (mixing[:, :, None] * grad_out.astype(jnp.float32)[:, None, :]).astype(
        jnp.bfloat16
    )
    scaled_flat = scaled_grad.reshape(-1, feature_dim)
    sent = jnp.zeros((1, slot_total, feature_dim), jnp.bfloat16).at[0, position].set(repeated)
    received = trade(sent, capacity)[0]
    gate_act, up_act, produced = expert_forward(received, w_gate, w_up, w_down)
    came_back = trade(produced[None], capacity)[0]
    sent_grad = (
        jnp.zeros((1, slot_total, feature_dim), jnp.bfloat16).at[0, position].set(scaled_flat)
    )
    received_grad = trade(sent_grad, capacity)[0]
    returned = expert_backward(received_grad, gate_act, up_act, w_gate, w_up, w_down)
    back_home = trade(returned[None], capacity)[0]
    out_rows = jnp.take(came_back, position, axis=0).reshape(row_count, topk, feature_dim)
    moe_out = jnp.sum(mixing[:, :, None] * out_rows.astype(jnp.float32), axis=1).astype(
        jnp.bfloat16
    )
    back_rows = jnp.take(back_home, position, axis=0).reshape(row_count, topk, feature_dim)
    scores = jnp.einsum("td,tkd->tk", grad_out, out_rows, preferred_element_type=jnp.float32)
    dlogit = mixing * (scores - jnp.sum(mixing * scores, axis=1, keepdims=True))
    onehot = (
        expert_ids[:, :, None] == jnp.arange(expert_count, dtype=jnp.int32)[None, None, :]
    ).astype(jnp.float32)
    dense = jnp.sum(onehot * dlogit[:, :, None], axis=1).astype(jnp.bfloat16)
    router_back = lax.dot_general(
        dense, router_weight, contract, preferred_element_type=jnp.float32
    )
    grad_tokens = (jnp.sum(back_rows.astype(jnp.float32), axis=1) + router_back).astype(
        jnp.bfloat16
    )
    router_part = lax.dot_general(
        tokens, dense, (((0,), (0,)), ((), ())), preferred_element_type=jnp.float32
    )
    router_grad = lax.psum(router_part, ("dp", "tp", "cp"))
    return (moe_out, grad_tokens, router_grad)


def solution(mesh):
    in_specs = (
        P(("dp", "tp", "cp"), None),
        P(("dp", "tp", "cp"), None),
        P(),
        P(("tp", "cp"), "dp", None),
        P(("tp", "cp"), "dp", None),
        P(("tp", "cp"), None, "dp"),
        P(("dp", "tp", "cp"), None),
    )
    out_specs = (P(("dp", "tp", "cp"), None), P(("dp", "tp", "cp"), None), P())
    return jax.shard_map(
        on_device, mesh=mesh, in_specs=in_specs, out_specs=out_specs, check_vma=False
    )
```

profile of v0, /device:TPU:1, one launch (start us, length us, event | category | flops | bytes accessed | tf_op | source)
XLA Modules:
  0.0 453.8 jit_solution(12045069232960749352)
XLA Ops:
  10.1 1.2 broadcast_in_dim.16
  11.6 1.9 scatter_custom_fusion
  13.5 1.2 reshape.105
  14.7 10.6 %all-to-all-start = ((bf16[1,32,12,1024]{3,2,0,1:T(8,128)(2,1)}), bf16[1,32,12,1024]{3,2,0,1:T(8,128)(2,1)S(1)}, u32[]{:S(2)}, u32[]{:S(2)}) async-start(bf16[1,32,12,1024]{3,2,0,1:T(8,128)(2,1)} %bitcast.4), calls=%async_computation | async-start | bytes 2097152 | tf_op jit(solution)/shard_map/all_to_all | solution.py:21
  25.3 27.5 %all-gather.2 = bf16[1,384,1024]{1,2,0:T(8,128)(2,1)} all-gather(bf16[1,384,64]{1,2,0:T(8,128)(2,1)S(1)} %copy-done.15), channel_id=4, replica_groups=mesh['dp'=16,'tp'=4,'cp'=8] {'dp'}, dimensions={2}, use_global_device_ids=true | all-gather | bytes 835584 | tf_op jit(solution)/shard_map/all_gather | solution.py:60
  52.9 16.6 %all-gather.1 = bf16[1,1024,384]{2,1,0:T(8,128)(2,1)S(1)} all-gather(bf16[1,64,384]{2,1,0:T(8,128)(2,1)S(1)} %copy-done.16), channel_id=3, replica_groups=mesh['dp'=16,'tp'=4,'cp'=8] {'dp'}, dimensions={1}, use_global_device_ids=true | all-gather | bytes 835584 | tf_op jit(solution)/shard_map/all_gather | solution.py:59
  69.5 17.9 %all-gather = bf16[1,1024,384]{2,1,0:T(8,128)(2,1)S(1)} all-gather(bf16[1,64,384]{2,1,0:T(8,128)(2,1)S(1)} %copy-done.17), channel_id=2, replica_groups=mesh['dp'=16,'tp'=4,'cp'=8] {'dp'}, dimensions={1}, use_global_device_ids=true | all-gather | bytes 835584 | tf_op jit(solution)/shard_map/all_gather | solution.py:58
  90.5 1.2 reshape_broadcast_in_dim.6
  91.8 9.6 %all-to-all-start.1 = ((bf16[1,32,12,1024]{3,2,0,1:T(8,128)(2,1)}), bf16[1,32,12,1024]{3,2,0,1:T(8,128)(2,1)S(1)}, u32[]{:S(2)}, u32[]{:S(2)}) async-start(bf16[1,32,12,1024]{3,2,0,1:T(8,128)(2,1)} %bitcast.8), calls=%async_computation.1 | async-start | bytes 2097152 | tf_op jit(solution)/shard_map/all_to_all | solution.py:21
  101.9 2.0 gather_fusion
  104.4 1.7 mul.98
  106.1 21.9 %all-to-all-done.1 = bf16[1,32,12,1024]{3,2,0,1:T(8,128)(2,1)S(1)} async-done(((bf16[1,32,12,1024]{3,2,0,1:T(8,128)(2,1)}), bf16[1,32,12,1024]{3,2,0,1:T(8,128)(2,1)S(1)}, u32[]{:S(2)}, u32[]{:S(2)}) %all-to-all-start.1) | async-done | bytes 786464 | tf_op jit(solution)/shard_map/all_to_all | solution.py:21
  128.3 1.2 gather_fusion.1
  131.3 2.0 scatter_custom_fusion.1
  133.5 33.6 %all_to_all.20 = bf16[1,32,12,1024]{3,2,0,1:T(8,128)(2,1)S(1)} all-to-all(bf16[1,32,12,1024]{3,2,0,1:T(8,128)(2,1)S(1)} %bitcast.72), channel_id=1, replica_groups=mesh['dp'=16,'tp'=4,'cp'=8] {'tp','cp'}, dimensions={1} | all-to-all | bytes 1572864 | tf_op jit(solution)/shard_map/all_to_all | solution.py:21
  167.3 1.8 fusion.1
  170.9 1.2 reshape_broadcast_in_dim.7
  172.1 6.0 %all-to-all-start.3 = ((bf16[1,32,12,1024]{3,2,0,1:T(8,128)(2,1)}), bf16[1,32,12,1024]{3,2,0,1:T(8,128)(2,1)S(1)}, u32[]{:S(2)}, u32[]{:S(2)}) async-start(bf16[1,32,12,1024]{3,2,0,1:T(8,128)(2,1)} %bitcast.10), calls=%async_computation.3 | async-start | bytes 2097152 | tf_op jit(solution)/shard_map/all_to_all | solution.py:21
  179.0 2.1 multiply_reduce_fusion
  181.2 22.9 %all-to-all-done.3 = bf16[1,32,12,1024]{3,2,0,1:T(8,128)(2,1)S(1)} async-done(((bf16[1,32,12,1024]{3,2,0,1:T(8,128)(2,1)}), bf16[1,32,12,1024]{3,2,0,1:T(8,128)(2,1)S(1)}, u32[]{:S(2)}, u32[]{:S(2)}) %all-to-all-start.3) | async-done | bytes 786464 | tf_op jit(solution)/shard_map/all_to_all | solution.py:21
  204.2 1.2 gather_fusion.2
  206.1 1.2 reduce_sum.60
  208.3 237.0 %all-reduce.3.cloned.1.call-done = f32[1024,32]{0,1:T(8,128)} async-done(((f32[1024,32]{0,1:T(8,128)}), f32[1024,32]{0,1:T(8,128)}) %all-reduce.3.cloned.1.call-update) | async-done | bytes 131088 | tf_op jit(solution)/shard_map/psum | solution.py:104
  445.3 1.6 copy.73
  (89 shorter events, 14.1 us)
Async XLA Ops:
  7.2 94.5 %copy-start = (bf16[1024,32]{0,1:T(8,128)(2,1)S(1)}, bf16[1024,32]{0,1:T(8,128)(2,1)}, u32[]{:S(2)}) copy-start(bf16[1024,32]{0,1:T(8,128)(2,1)} %param.11) | copy-start | bytes 196612
  13.5 11.8 %copy-start.15 = (bf16[1,384,64]{1,2,0:T(8,128)(2,1)S(1)}, bf16[1,384,64]{1,2,0:T(8,128)(2,1)}, u32[]{:S(2)}) copy-start(bf16[1,384,64]{1,2,0:T(8,128)(2,1)} %param.14) | copy-start | bytes 147460
  14.7 38.2 %copy-start.16 = (bf16[1,64,384]{2,1,0:T(8,128)(2,1)S(1)}, bf16[1,64,384]{2,1,0:T(8,128)(2,1)}, u32[]{:S(2)}) copy-start(bf16[1,64,384]{2,1,0:T(8,128)(2,1)} %param.13) | copy-start | bytes 147460
  14.7 54.8 %copy-start.17 = (bf16[1,64,384]{2,1,0:T(8,128)(2,1)S(1)}, bf16[1,64,384]{2,1,0:T(8,128)(2,1)}, u32[]{:S(2)}) copy-start(bf16[1,64,384]{2,1,0:T(8,128)(2,1)} %param.12) | copy-start | bytes 147460
  14.7 72.7 %all-to-all-start = ((bf16[1,32,12,1024]{3,2,0,1:T(8,128)(2,1)}), bf16[1,32,12,1024]{3,2,0,1:T(8,128)(2,1)S(1)}, u32[]{:S(2)}, u32[]{:S(2)}) async-start(bf16[1,32,12,1024]{3,2,0,1:T(8,128)(2,1)} %bitcast.4), calls=%async_computation | async-start | bytes 2097152 | tf_op jit(solution)/shard_map/all_to_all | solution.py:21
  69.5 18.7 %copy-start.2 = (bf16[1,1024,384]{2,1,0:T(8,128)(2,1)}, bf16[1,1024,384]{2,1,0:T(8,128)(2,1)S(1)}, u32[]{:S(2)}) copy-start(bf16[1,1024,384]{2,1,0:T(8,128)(2,1)S(1)} %all-gather.1) | copy-start | bytes 2359300
  87.4 0.9 copy-start.4
  88.3 0.8 copy-start.12
  88.3 1.6 copy-start.6
  89.1 0.8 copy-start.10
  90.5 10.9 %copy-start.18 = (s32[128,2]{0,1:T(2,128)S(1)}, s32[128,2]{0,1:T(2,128)}, u32[]{:S(2)}) copy-start(s32[128,2]{0,1:T(2,128)} %param.10) | copy-start | bytes 3076
  91.8 9.9 %copy-start.7 = (bf16[128,1024]{1,0:T(8,128)(2,1)S(1)}, bf16[128,1024]{1,0:T(8,128)(2,1)}, u32[]{:S(2)}) copy-start(bf16[128,1024]{1,0:T(8,128)(2,1)} %param.9) | copy-start | bytes 786436
  91.8 36.3 %all-to-all-start.1 = ((bf16[1,32,12,1024]{3,2,0,1:T(8,128)(2,1)}), bf16[1,32,12,1024]{3,2,0,1:T(8,128)(2,1)S(1)}, u32[]{:S(2)}, u32[]{:S(2)}) async-start(bf16[1,32,12,1024]{3,2,0,1:T(8,128)(2,1)} %bitcast.8), calls=%async_computation.1 | async-start | bytes 2097152 | tf_op jit(solution)/shard_map/all_to_all | solution.py:21
  101.9 2.2 copy-start.14
  129.8 1.2 copy-start.8
  129.8 1.5 copy-start.1
  167.1 2.0 copy-start.5
  167.3 1.8 copy-start.11
  167.3 1.8 copy-start.13
  169.1 1.1 copy-start.3
  172.1 6.9 %copy-start.9 = (bf16[128,2,1024]{2,1,0:T(2,128)(2,1)S(1)}, bf16[128,2,1024]{2,1,0:T(2,128)(2,1)}, u32[]{:S(2)}) copy-start(bf16[128,2,1024]{2,1,0:T(2,128)(2,1)} %copy-done.8) | copy-start | bytes 1572868
  172.1 32.0 %all-to-all-start.3 = ((bf16[1,32,12,1024]{3,2,0,1:T(8,128)(2,1)}), bf16[1,32,12,1024]{3,2,0,1:T(8,128)(2,1)S(1)}, u32[]{:S(2)}, u32[]{:S(2)}) async-start(bf16[1,32,12,1024]{3,2,0,1:T(8,128)(2,1)} %bitcast.10), calls=%async_computation.3 | async-start | bytes 2097152 | tf_op jit(solution)/shard_map/all_to_all | solution.py:21
  178.1 267.3 %all-reduce.3.cloned.1.call-start = ((), (), s32[]{:S(2)}) async-start(), calls=%async_computation.4 | async-start | bytes 262144 | tf_op jit(solution)/shard_map/psum | solution.py:104
Sparse Core Ops, SparseCore 0:
  184.5 260.8 all-reduce.2
where the time goes:
time: 454 us
  waiting for transfers between devices  282 us (62%)
  blocking collectives  95.7 us (21%)
  starting transfers between devices  26.3 us (6%)
  local copies, waits for them, and re-layouts  20.4 us (4%)
  between operations  14.4 us (3%)
  matrix products  7.95 us (2%)
  other arithmetic  7.16 us (2%)
    psum x1, waiting for transfers between devices, on_device(): router_grad = lax.psum(router_part, ('dp', 'tp', 'cp'))  237 us
    all_to_all x3, waiting for transfers between devices, trade(): lax.all_to_all(shaped, ('tp', 'cp'), split_axis=1, concat_axis=1, tiled=T...  44.8 us
    all_to_all x1, blocking collectives, trade(): lax.all_to_all(shaped, ('tp', 'cp'), split_axis=1, concat_axis=1, tiled=T...  33.6 us
    all_gather x1, blocking collectives, on_device(): lax.all_gather(down_weight[0], 'dp', axis=1, tiled=True)  27.5 us
    all_to_all x3, starting transfers between devices, trade(): lax.all_to_all(shaped, ('tp', 'cp'), split_axis=1, concat_axis=1, tiled=T...  26.3 us
    all_gather x1, blocking collectives, on_device(): lax.all_gather(gate_weight[0], 'dp', axis=0, tiled=True)  17.9 us
    all_gather x1, blocking collectives, on_device(): lax.all_gather(up_weight[0], 'dp', axis=0, tiled=True)  16.6 us
  transfers between devices with their start and end apart: 4, of which 3 were waited for; matrix products, arithmetic and copies ran while one was open for 3% of the time, Pallas kernels for 0%

commit v1 on v0

--- a/solution.py
+++ b/solution.py
@@ -101,7 +101,7 @@
     router_part = lax.dot_general(
         tokens, dense, (((0,), (0,)), ((), ())), preferred_element_type=jnp.float32
     )
-    router_grad = lax.psum(router_part, ("dp", "tp", "cp"))
+    router_grad = lax.psum(lax.psum(router_part, "dp"), ("tp", "cp"))
     return (moe_out, grad_tokens, router_grad)
 
 

time: 454 us -> 459 us (1.011)
    psum x1 -> x2, waiting for transfers between devices: 237 us -> 261 us  [on_device(): router_grad = lax.psum(lax.psum(router_part, 'dp'), ('tp', 'cp'))]
    all_to_all x3, waiting for transfers between devices: 44.8 us -> 22 us  [trade(): lax.all_to_all(shaped, ('tp', 'cp'), split_axis=1, concat_axis=1, tiled=T...]
  transfers between devices with their start and end apart: 4 -> 5, of which waited for: 3 -> 3; matrix products, arithmetic and copies ran while one was open for 3% -> 3% of each run, Pallas kernels for 0% -> 0%
where the time goes in v1:
time: 459 us; the launch traced here: 455 us
  waiting for transfers between devices  283 us (62%)
  blocking collectives  95.7 us (21%)
  starting transfers between devices  26.3 us (6%)
  local copies, waits for them, and re-layouts  20.4 us (4%)
  between operations  14.5 us (3%)
  matrix products  7.95 us (2%)
  other arithmetic  7.16 us (2%)
    psum x2, waiting for transfers between devices, on_device(): router_grad = lax.psum(lax.psum(router_part, 'dp'), ('tp', 'cp'))  261 us
    all_to_all x1, blocking collectives, trade(): lax.all_to_all(shaped, ('tp', 'cp'), split_axis=1, concat_axis=1, tiled=T...  33.6 us
    all_gather x1, blocking collectives, on_device(): lax.all_gather(down_weight[0], 'dp', axis=1, tiled=True)  27.5 us
    all_to_all x3, starting transfers between devices, trade(): lax.all_to_all(shaped, ('tp', 'cp'), split_axis=1, concat_axis=1, tiled=T...  26.3 us
    all_to_all x3, waiting for transfers between devices, trade(): lax.all_to_all(shaped, ('tp', 'cp'), split_axis=1, concat_axis=1, tiled=T...  22 us
    all_gather x1, blocking collectives, on_device(): lax.all_gather(gate_weight[0], 'dp', axis=0, tiled=True)  17.9 us
    all_gather x1, blocking collectives, on_device(): lax.all_gather(up_weight[0], 'dp', axis=0, tiled=True)  16.6 us
  transfers between devices with their start and end apart: 5, of which 3 were waited for; matrix products, arithmetic and copies ran while one was open for 3% of the time, Pallas kernels for 0%

profile of v1, /device:TPU:1, one launch (start us, length us, event | category | flops | bytes accessed | tf_op | source)
XLA Modules:
  0.0 455.0 jit_solution(10569930727687870523)
XLA Ops:
  10.1 1.2 broadcast_in_dim.16
  11.6 1.9 scatter_custom_fusion
  13.5 1.2 reshape.105
  14.7 10.6 %all-to-all-start = ((bf16[1,32,12,1024]{3,2,0,1:T(8,128)(2,1)}), bf16[1,32,12,1024]{3,2,0,1:T(8,128)(2,1)S(1)}, u32[]{:S(2)}, u32[]{:S(2)}) async-start(bf16[1,32,12,1024]{3,2,0,1:T(8,128)(2,1)} %bitcast.4), calls=%async_computation | async-start | bytes 2097152 | tf_op jit(solution)/shard_map/all_to_all | solution.py:21
  25.3 27.5 %all-gather.2 = bf16[1,384,1024]{1,2,0:T(8,128)(2,1)} all-gather(bf16[1,384,64]{1,2,0:T(8,128)(2,1)S(1)} %copy-done.15), channel_id=4, replica_groups=mesh['dp'=16,'tp'=4,'cp'=8] {'dp'}, dimensions={2}, use_global_device_ids=true | all-gather | bytes 835584 | tf_op jit(solution)/shard_map/all_gather | solution.py:60
  52.9 16.6 %all-gather.1 = bf16[1,1024,384]{2,1,0:T(8,128)(2,1)S(1)} all-gather(bf16[1,64,384]{2,1,0:T(8,128)(2,1)S(1)} %copy-done.16), channel_id=3, replica_groups=mesh['dp'=16,'tp'=4,'cp'=8] {'dp'}, dimensions={1}, use_global_device_ids=true | all-gather | bytes 835584 | tf_op jit(solution)/shard_map/all_gather | solution.py:59
  69.5 17.9 %all-gather = bf16[1,1024,384]{2,1,0:T(8,128)(2,1)S(1)} all-gather(bf16[1,64,384]{2,1,0:T(8,128)(2,1)S(1)} %copy-done.17), channel_id=2, replica_groups=mesh['dp'=16,'tp'=4,'cp'=8] {'dp'}, dimensions={1}, use_global_device_ids=true | all-gather | bytes 835584 | tf_op jit(solution)/shard_map/all_gather | solution.py:58
  90.5 1.2 reshape_broadcast_in_dim.6
  91.8 9.6 %all-to-all-start.1 = ((bf16[1,32,12,1024]{3,2,0,1:T(8,128)(2,1)}), bf16[1,32,12,1024]{3,2,0,1:T(8,128)(2,1)S(1)}, u32[]{:S(2)}, u32[]{:S(2)}) async-start(bf16[1,32,12,1024]{3,2,0,1:T(8,128)(2,1)} %bitcast.8), calls=%async_computation.1 | async-start | bytes 2097152 | tf_op jit(solution)/shard_map/all_to_all | solution.py:21
  101.9 2.0 gather_fusion
  104.4 1.7 mul.98
  106.1 21.9 %all-to-all-done.1 = bf16[1,32,12,1024]{3,2,0,1:T(8,128)(2,1)S(1)} async-done(((bf16[1,32,12,1024]{3,2,0,1:T(8,128)(2,1)}), bf16[1,32,12,1024]{3,2,0,1:T(8,128)(2,1)S(1)}, u32[]{:S(2)}, u32[]{:S(2)}) %all-to-all-start.1) | async-done | bytes 786464 | tf_op jit(solution)/shard_map/all_to_all | solution.py:21
  128.3 1.2 gather_fusion.1
  131.3 2.0 scatter_custom_fusion.1
  133.5 33.6 %all_to_all.20 = bf16[1,32,12,1024]{3,2,0,1:T(8,128)(2,1)S(1)} all-to-all(bf16[1,32,12,1024]{3,2,0,1:T(8,128)(2,1)S(1)} %bitcast.72), channel_id=1, replica_groups=mesh['dp'=16,'tp'=4,'cp'=8] {'tp','cp'}, dimensions={1} | all-to-all | bytes 1572864 | tf_op jit(solution)/shard_map/all_to_all | solution.py:21
  167.3 1.8 fusion.1
  170.9 1.2 reshape_broadcast_in_dim.7
  172.1 6.0 %all-to-all-start.3 = ((bf16[1,32,12,1024]{3,2,0,1:T(8,128)(2,1)}), bf16[1,32,12,1024]{3,2,0,1:T(8,128)(2,1)S(1)}, u32[]{:S(2)}, u32[]{:S(2)}) async-start(bf16[1,32,12,1024]{3,2,0,1:T(8,128)(2,1)} %bitcast.10), calls=%async_computation.3 | async-start | bytes 2097152 | tf_op jit(solution)/shard_map/all_to_all | solution.py:21
  179.1 2.1 multiply_reduce_fusion
  181.2 113.6 %all-reduce.4.cloned.1.call-done = f32[1024,32]{0,1:T(8,128)} async-done(((f32[1024,32]{0,1:T(8,128)}), f32[1024,32]{0,1:T(8,128)}) %all-reduce.4.cloned.1.call-update) | async-done | bytes 131088 | tf_op jit(solution)/shard_map/psum | solution.py:104
  295.0 1.2 gather_fusion.2
  297.0 1.2 reduce_sum.60
  299.2 147.4 %all-reduce.6.cloned.1.call-done = f32[1024,32]{0,1:T(8,128)} async-done(((f32[1024,32]{0,1:T(8,128)}), f32[1024,32]{0,1:T(8,128)}) %all-reduce.6.cloned.1.call-update) | async-done | bytes 131088 | tf_op jit(solution)/shard_map/psum | solution.py:104
  446.6 1.6 copy.74
  (92 shorter events, 14.2 us)
Async XLA Ops:
  7.2 94.5 %copy-start = (bf16[1024,32]{0,1:T(8,128)(2,1)S(1)}, bf16[1024,32]{0,1:T(8,128)(2,1)}, u32[]{:S(2)}) copy-start(bf16[1024,32]{0,1:T(8,128)(2,1)} %param.11) | copy-start | bytes 196612
  13.5 11.8 %copy-start.15 = (bf16[1,384,64]{1,2,0:T(8,128)(2,1)S(1)}, bf16[1,384,64]{1,2,0:T(8,128)(2,1)}, u32[]{:S(2)}) copy-start(bf16[1,384,64]{1,2,0:T(8,128)(2,1)} %param.14) | copy-start | bytes 147460
  14.7 38.2 %copy-start.16 = (bf16[1,64,384]{2,1,0:T(8,128)(2,1)S(1)}, bf16[1,64,384]{2,1,0:T(8,128)(2,1)}, u32[]{:S(2)}) copy-start(bf16[1,64,384]{2,1,0:T(8,128)(2,1)} %param.13) | copy-start | bytes 147460
  14.7 54.8 %copy-start.17 = (bf16[1,64,384]{2,1,0:T(8,128)(2,1)S(1)}, bf16[1,64,384]{2,1,0:T(8,128)(2,1)}, u32[]{:S(2)}) copy-start(bf16[1,64,384]{2,1,0:T(8,128)(2,1)} %param.12) | copy-start | bytes 147460
  14.7 72.7 %all-to-all-start = ((bf16[1,32,12,1024]{3,2,0,1:T(8,128)(2,1)}), bf16[1,32,12,1024]{3,2,0,1:T(8,128)(2,1)S(1)}, u32[]{:S(2)}, u32[]{:S(2)}) async-start(bf16[1,32,12,1024]{3,2,0,1:T(8,128)(2,1)} %bitcast.4), calls=%async_computation | async-start | bytes 2097152 | tf_op jit(solution)/shard_map/all_to_all | solution.py:21
  69.5 18.7 %copy-start.2 = (bf16[1,1024,384]{2,1,0:T(8,128)(2,1)}, bf16[1,1024,384]{2,1,0:T(8,128)(2,1)S(1)}, u32[]{:S(2)}) copy-start(bf16[1,1024,384]{2,1,0:T(8,128)(2,1)S(1)} %all-gather.1) | copy-start | bytes 2359300
  87.4 0.9 copy-start.4
  88.3 0.8 copy-start.12
  88.3 1.6 copy-start.6
  89.1 0.8 copy-start.10
  90.5 10.9 %copy-start.18 = (s32[128,2]{0,1:T(2,128)S(1)}, s32[128,2]{0,1:T(2,128)}, u32[]{:S(2)}) copy-start(s32[128,2]{0,1:T(2,128)} %param.10) | copy-start | bytes 3076
  91.8 9.9 %copy-start.7 = (bf16[128,1024]{1,0:T(8,128)(2,1)S(1)}, bf16[128,1024]{1,0:T(8,128)(2,1)}, u32[]{:S(2)}) copy-start(bf16[128,1024]{1,0:T(8,128)(2,1)} %param.9) | copy-start | bytes 786436
  91.8 36.3 %all-to-all-start.1 = ((bf16[1,32,12,1024]{3,2,0,1:T(8,128)(2,1)}), bf16[1,32,12,1024]{3,2,0,1:T(8,128)(2,1)S(1)}, u32[]{:S(2)}, u32[]{:S(2)}) async-start(bf16[1,32,12,1024]{3,2,0,1:T(8,128)(2,1)} %bitcast.8), calls=%async_computation.1 | async-start | bytes 2097152 | tf_op jit(solution)/shard_map/all_to_all | solution.py:21
  101.9 2.2 copy-start.14
  129.8 1.2 copy-start.8
  129.8 1.5 copy-start.1
  167.1 2.0 copy-start.5
  167.3 1.8 copy-start.11
  167.3 1.8 copy-start.13
  169.1 1.1 copy-start.3
  172.1 7.0 %copy-start.9 = (bf16[128,2,1024]{2,1,0:T(2,128)(2,1)S(1)}, bf16[128,2,1024]{2,1,0:T(2,128)(2,1)}, u32[]{:S(2)}) copy-start(bf16[128,2,1024]{2,1,0:T(2,128)(2,1)} %copy-done.8) | copy-start | bytes 1572868
  172.1 122.8 %all-to-all-start.3 = ((bf16[1,32,12,1024]{3,2,0,1:T(8,128)(2,1)}), bf16[1,32,12,1024]{3,2,0,1:T(8,128)(2,1)S(1)}, u32[]{:S(2)}, u32[]{:S(2)}) async-start(bf16[1,32,12,1024]{3,2,0,1:T(8,128)(2,1)} %bitcast.10), calls=%async_computation.3 | async-start | bytes 2097152 | tf_op jit(solution)/shard_map/all_to_all | solution.py:21
  178.1 116.7 %all-reduce.4.cloned.1.call-start = ((), (), s32[]{:S(2)}) async-start(), calls=%async_computation.4 | async-start | bytes 262144 | tf_op jit(solution)/shard_map/psum | solution.py:104
  179.0 267.6 %all-reduce.6.cloned.1.call-start = ((), (), s32[]{:S(2)}) async-start(), calls=%async_computation.5 | async-start | bytes 262144 | tf_op jit(solution)/shard_map/psum | solution.py:104
Sparse Core Ops, SparseCore 0:
  181.8 112.9 all-reduce.3
  298.7 147.9 all-reduce.5
